TPU v7x, 32 devices: a whole 2x2x4 slice. The times are simulated.
32 devices in a mesh: line: 4 (over z), tx: 2 (over core), ty: 4 (over y, x).
Axes of the slice: x: 2, y: 2, z: 4, core: 2. Of those that a mesh axis runs over, the one named last changes fastest.
Arguments:
- right_side: float32 [16, 8, 16, 128], P('line', 'tx', 'ty'), may hold values from -3 to 3
- start_field: float32 [16, 8, 16, 128], P('line', 'tx', 'ty'), may hold values from -3 to 3
- line_inverse: bfloat16 [16, 8, 16, 128, 128], P('line', 'tx', 'ty'), as said below
- lower_scale: float32 [16, 8, 16], P('line', 'tx', 'ty'), may hold values from 0.85 to 1
- upper_scale: float32 [16, 8, 16], P('line', 'tx', 'ty'), may hold values from 0.85 to 1
- lower_block: float32 [128, 128], replicated
- upper_block: float32 [128, 128], replicated
- face_blocks: float32 [4, 128, 128], replicated, may hold values from -0.15625 to 0.15625
- face_kind: int32 [4, 16, 8, 16], P(None, 'line', 'tx', 'ty'), may hold values from 0 to 3
- face_scale: float32 [4, 16, 8, 16], P(None, 'line', 'tx', 'ty'), may hold values from 0.25 to 1
- agglomerate: int32 [16, 8, 16], P('line', 'tx', 'ty'), may hold values from 0 to 63
- restriction: float32 [32, 128], replicated, may hold values from -0.5 to 0.5
- coarse_inverse: float32 [4, 2, 64, 32, 32], P('line', 'tx', 'ty'), as said below
Outputs:
- corrected: float32 [16, 8, 16, 128], P('line', 'tx', 'ty')
- residual: float32 [16, 8, 16, 128], P('line', 'tx', 'ty')
Inputs may be any that keep to these rules, and one draw needn't show every extreme that they name: An element's agglomerate is one of the 64 agglomerates of its own column. `line_inverse`: each block is a diagonal of positive entries plus a full-rank part. `coarse_inverse`: each block is a diagonal of positive entries plus a full-rank part.
All inputs are finite; a program needn't handle non-finite values.
Results may differ from a plain program's by a relative error of at most 0.0003.
Values sent between devices are 32-bit elements; how exact they have to be, the bound alone decides.
A program may use at most 64 MiB of HBM per device.

v0:
```python
import jax
import jax.numpy as jnp
from jax import lax
from jax.sharding import PartitionSpec as P

SWEEPS = 2


highest = lax.Precision.HIGHEST


def padded_2(array, sides, width):
    for axis, dim in sides:
        count, length = (lax.axis_size(axis), array.shape[dim])
        up = [(i, (i + 1) % count) for i in range(count - 1)]
        down = [(j, i) for i, j in up]
        last = lax.slice_in_dim(array, length - width, length, axis=dim)
        leading = lax.slice_in_dim(array, 0, width, axis=dim)
        before = lax.ppermute(last, axis, up)
        after = lax.ppermute(leading, axis, down)
        array = jnp.concatenate([before, array, after], axis=dim)
    return array


def from_behind(value, axis, steps):
    count = lax.axis_size(axis)
    leading, last = (max(0, -steps), min(count, count - steps))
    return lax.ppermute(value, axis, [(source, source + steps) for source in range(leading, last)])


def couple(field, face_blocks, face_kind, face_scale):
    padded = padded_2(field, (("tx", 1), ("ty", 2)), 1)
    beside = (padded[:, :-2, 1:-1], padded[:, 2:, 1:-1], padded[:, 1:-1, :-2], padded[:, 1:-1, 2:])
    total = jnp.zeros_like(field)
    kinds = jnp.arange(4, dtype=jnp.int32)
    for side in range(4):
        images = jnp.einsum("sxyb,kcb->ksxyc", beside[side], face_blocks, precision=highest)
        chosen = (face_kind[side][None] == kinds[:, None, None, None]).astype(jnp.float32)
        picked = jnp.sum(chosen[..., None] * images, axis=0)
        total = total + face_scale[side][..., None] * picked
    return total


def forward(line_inverse, lower_scale, lower_block, drive, start):

    def forward_step(carry, items):
        inverse, scale, source = items
        inner = source - scale[..., None] * jnp.einsum(
            "cb,xyb->xyc", lower_block, carry, precision=highest
        )
        value = jnp.einsum("xycb,xyb->xyc", inverse.astype(jnp.float32), inner, precision=highest)
        return (value, value)

    final, values = lax.scan(forward_step, start, (line_inverse, lower_scale, drive))
    return values


def backward(line_inverse, upper_scale, upper_block, ahead, start):

    def backward_step(carry, items):
        inverse, scale, source = items
        inner = scale[..., None] * jnp.einsum("cb,xyb->xyc", upper_block, carry, precision=highest)
        value = source - jnp.einsum(
            "xycb,xyb->xyc", inverse.astype(jnp.float32), inner, precision=highest
        )
        return (value, value)

    final, values = lax.scan(backward_step, start, (line_inverse, upper_scale, ahead), reverse=True)
    return values


def body(
    right_side,
    start_field,
    line_inverse,
    lower_scale,
    upper_scale,
    lower_block,
    upper_block,
    face_blocks,
    face_kind,
    face_scale,
    agglomerate,
    restriction,
    coarse_inverse,
):
    width = right_side.shape[-1]
    empty = jnp.zeros(right_side.shape[1:], jnp.float32)
    segments = lax.axis_size("line")
    field = start_field
    previous = start_field
    for sweep in range(SWEEPS):
        previous = field
        drive = right_side - couple(previous, face_blocks, face_kind, face_scale)
        incoming = empty
        for turn in range(segments - 1):
            ahead = forward(line_inverse, lower_scale, lower_block, drive, incoming)
            incoming = from_behind(ahead[-1], "line", 1)
        ahead = forward(line_inverse, lower_scale, lower_block, drive, incoming)
        arriving = empty
        for turn in range(segments - 1):
            behind = backward(line_inverse, upper_scale, upper_block, ahead, arriving)
            arriving = from_behind(behind[0], "line", -1)
        field = backward(line_inverse, upper_scale, upper_block, ahead, arriving)
    residual = couple(previous - field, face_blocks, face_kind, face_scale)
    owned_count = coarse_inverse.shape[2]
    total_aggs = owned_count * lax.axis_size("ty")
    flat = residual.reshape(-1, width)
    projected = jnp.einsum("cb,eb->ec", restriction, flat, precision=highest)
    chosen = (
        agglomerate.reshape(-1)[:, None] == jnp.arange(total_aggs, dtype=jnp.int32)[None, :]
    ).astype(jnp.float32)
    partial_value = jnp.einsum("ea,ec->ac", chosen, projected, precision=highest)
    owned = lax.psum_scatter(partial_value, "ty", scatter_dimension=0, tiled=True)
    update = jnp.einsum("acd,ad->ac", coarse_inverse[0, 0], owned, precision=highest)
    spread = jnp.einsum(
        "ea,ac->ec", chosen, lax.all_gather(update, "ty", axis=0, tiled=True), precision=highest
    )
    fine = jnp.einsum("cb,ec->eb", restriction, spread, precision=highest).reshape(residual.shape)
    return (field + fine, residual)


def solution(mesh):
    in_specs = (
        P("line", "tx", "ty", None),
        P("line", "tx", "ty", None),
        P("line", "tx", "ty", None, None),
        P("line", "tx", "ty"),
        P("line", "tx", "ty"),
        P(),
        P(),
        P(),
        P(None, "line", "tx", "ty"),
        P(None, "line", "tx", "ty"),
        P("line", "tx", "ty"),
        P(),
        P("line", "tx", "ty", None, None),
    )
    out_specs = (P("line", "tx", "ty", None), P("line", "tx", "ty", None))
    return jax.shard_map(body, mesh=mesh, in_specs=in_specs, out_specs=out_specs, check_vma=False)
```

profile of v0, /device:TPU:0, one launch (start us, length us, event | category | flops | bytes accessed | tf_op | source)
XLA Modules:
  0.0 216.5 jit_solution(16443821743586129277)
XLA Ops:
  7.5 4.2 %collective-permute-start.2 = (f32[4,6,1,128]{3,2,1,0:T(1,128)S(1)}, f32[4,6,1,128]{3,2,1,0:T(1,128)S(1)}, u32[]{:S(2)}, u32[]{:S(2)}) collective-permute-start(f32[4,6,1,128]{3,2,1,0:T(1,128)S(1)} %get-tuple-element.1734), channel_id=1, source_target_pairs={{0,1},{1,2},{2,3},{4,5},{5,6},{6,7},{8,9},{9,10},{10,11},{12,13},{... | collective-permute-start | bytes 36872 | tf_op jit(solution)/shard_map/ppermute | solution.py:19
  18.0 4.7 %while.226 = (s32[]{:T(128)}, f32[4,4,128]{2,1,0:T(4,128)S(1)}, f32[4,4,4,128]{3,2,1,0:T(4,128)S(1)}, bf16[4,4,4,128,128]{4,3,2,1,0:T(8,128)(2,1)S(1)}, f32[4,4,...) while((s32[]{:T(128)}, f32[4,4,128]{2,1,0:T(4,128)S(1)}, ...), condition=%wide.region_5.6_spmd, body=%wide.region_4.5_spmd.sunk | while | flops 6295554 | bytes 647461 | solution.py:54
  27.6 4.7 %while.227 = (s32[]{:T(128)}, f32[4,4,128]{2,1,0:T(4,128)S(1)}, f32[4,4,4,128]{3,2,1,0:T(4,128)S(1)}, bf16[4,4,4,128,128]{4,3,2,1,0:T(8,128)(2,1)S(1)}, f32[4,4,...) while((s32[]{:T(128)}, f32[4,4,128]{2,1,0:T(4,128)S(1)}, ...), condition=%wide.region_7.8_spmd, body=%wide.region_6.7_spmd.sunk | while | flops 6295554 | bytes 647461 | solution.py:54
  32.3 4.2 %collective-permute-start.5 = (f32[4,4,128]{2,1,0:T(4,128)S(1)}, f32[4,4,128]{2,1,0:T(4,128)S(1)}, u32[]{:S(2)}, u32[]{:S(2)}) collective-permute-start(f32[4,4,128]{2,1,0:T(4,128)S(1)} %slice_bitcast_fusion.10), channel_id=1, source_target_pairs={{0,8},{8,16},{16,24},{1,9},{9,17},{17,25},{2,10},{10,18},{18,26},{... | collective-permute-start | bytes 24584 | tf_op jit(solution)/shard_map/ppermute | solution.py:28
  37.8 4.7 %while.228 = (s32[]{:T(128)}, f32[4,4,128]{2,1,0:T(4,128)S(1)}, f32[4,4,4,128]{3,2,1,0:T(4,128)S(1)}, bf16[4,4,4,128,128]{4,3,2,1,0:T(8,128)(2,1)S(1)}, f32[4,4,...) while((s32[]{:T(128)}, f32[4,4,128]{2,1,0:T(4,128)S(1)}, ...), condition=%wide.region_9.10_spmd, body=%wide.region_8.9_spmd.sunk | while | flops 6295554 | bytes 647461 | solution.py:54
  42.6 4.3 %collective-permute-start.6 = (f32[4,4,128]{2,1,0:T(4,128)S(1)}, f32[4,4,128]{2,1,0:T(4,128)S(1)}, u32[]{:S(2)}, u32[]{:S(2)}) collective-permute-start(f32[4,4,128]{2,1,0:T(4,128)S(1)} %slice_bitcast_fusion.9), channel_id=1, source_target_pairs={{0,8},{8,16},{16,24},{1,9},{9,17},{17,25},{2,10},{10,18},{18,26},{... | collective-permute-start | bytes 24584 | tf_op jit(solution)/shard_map/ppermute | solution.py:28
  48.3 4.7 %while.229 = (s32[]{:T(128)}, f32[4,4,128]{2,1,0:T(4,128)S(1)}, f32[4,4,4,128]{3,2,1,0:T(4,128)S(1)}, bf16[4,4,4,128,128]{4,3,2,1,0:T(8,128)(2,1)S(1)}, f32[4,4,...) while((s32[]{:T(128)}, f32[4,4,128]{2,1,0:T(4,128)S(1)}, ...), condition=%wide.region_11.12_spmd, body=%wide.region_10.11_spmd.sunk | while | flops 6295554 | bytes 647461 | solution.py:54
  53.0 4.9 %while.240 = (s32[]{:T(128)}, f32[4,4,128]{2,1,0:T(4,128)S(1)}, f32[4,4,4,128]{3,2,1,0:T(4,128)S(1)}, f32[4,4,4,128]{3,2,1,0:T(4,128)S(1)}, bf16[4,4,4,128,128]{...) while((s32[]{:T(128)}, f32[4,4,128]{2,1,0:T(4,128)S(1)}, ...), condition=%wide.region_13.14_spmd.clone, body=%wide.region_12.13_spmd.clone.sunk | while | flops 6297604 | bytes 655687 | solution.py:68
  59.2 4.5 %collective-permute-done.7 = f32[4,4,128]{2,1,0:T(4,128)S(1)} collective-permute-done((f32[4,4,128]{2,1,0:T(4,128)S(1)}, f32[4,4,128]{2,1,0:T(4,128)S(1)}, u32[]{:S(2)}, u32[]{:S(2)}) %collective-permute-start.7) | collective-permute-done | bytes 8224 | tf_op jit(solution)/shard_map/ppermute | solution.py:28
  63.7 4.8 %while.230 = (s32[]{:T(128)}, f32[4,4,128]{2,1,0:T(4,128)S(1)}, f32[4,4,4,128]{3,2,1,0:T(4,128)S(1)}, f32[4,4,4,128]{3,2,1,0:T(4,128)S(1)}, bf16[4,4,4,128,128]{...) while((s32[]{:T(128)}, f32[4,4,128]{2,1,0:T(4,128)S(1)}, ...), condition=%wide.region_15.16_spmd, body=%wide.region_14.15_spmd.sunk | while | flops 6295555 | bytes 655669 | solution.py:68
  69.9 4.2 %collective-permute-done.8 = f32[4,4,128]{2,1,0:T(4,128)S(1)} collective-permute-done((f32[4,4,128]{2,1,0:T(4,128)S(1)}, f32[4,4,128]{2,1,0:T(4,128)S(1)}, u32[]{:S(2)}, u32[]{:S(2)}) %collective-permute-start.8) | collective-permute-done | bytes 8224 | tf_op jit(solution)/shard_map/ppermute | solution.py:28
  74.1 4.8 %while.231 = (s32[]{:T(128)}, f32[4,4,128]{2,1,0:T(4,128)S(1)}, f32[4,4,4,128]{3,2,1,0:T(4,128)S(1)}, f32[4,4,4,128]{3,2,1,0:T(4,128)S(1)}, bf16[4,4,4,128,128]{...) while((s32[]{:T(128)}, f32[4,4,128]{2,1,0:T(4,128)S(1)}, ...), condition=%wide.region_17.18_spmd, body=%wide.region_16.17_spmd.sunk | while | flops 6295555 | bytes 655669 | solution.py:68
  80.2 4.2 %collective-permute-done.9 = f32[4,4,128]{2,1,0:T(4,128)S(1)} collective-permute-done((f32[4,4,128]{2,1,0:T(4,128)S(1)}, f32[4,4,128]{2,1,0:T(4,128)S(1)}, u32[]{:S(2)}, u32[]{:S(2)}) %collective-permute-start.9) | collective-permute-done | bytes 8224 | tf_op jit(solution)/shard_map/ppermute | solution.py:28
  84.5 4.8 %while.232 = (s32[]{:T(128)}, f32[4,4,128]{2,1,0:T(4,128)S(1)}, f32[4,4,4,128]{3,2,1,0:T(4,128)S(1)}, f32[4,4,4,128]{3,2,1,0:T(4,128)S(1)}, bf16[4,4,4,128,128]{...) while((s32[]{:T(128)}, f32[4,4,128]{2,1,0:T(4,128)S(1)}, ...), condition=%wide.region_19.20_spmd, body=%wide.region_18.19_spmd.sunk | while | flops 6295555 | bytes 655669 | solution.py:68
  93.7 4.3 %collective-permute-start.12 = (f32[4,6,1,128]{3,2,1,0:T(1,128)S(1)}, f32[4,6,1,128]{3,2,1,0:T(1,128)S(1)}, u32[]{:S(2)}, u32[]{:S(2)}) collective-permute-start(f32[4,6,1,128]{3,2,1,0:T(1,128)S(1)} %get-tuple-element.1732), channel_id=1, source_target_pairs={{0,1},{1,2},{2,3},{4,5},{5,6},{6,7},{8,9},{9,10},{10,11},{12,13},{... | collective-permute-start | bytes 36872 | tf_op jit(solution)/shard_map/ppermute | solution.py:19
  104.2 4.7 %while.233 = (s32[]{:T(128)}, f32[4,4,128]{2,1,0:T(4,128)S(1)}, f32[4,4,4,128]{3,2,1,0:T(4,128)S(1)}, bf16[4,4,4,128,128]{4,3,2,1,0:T(8,128)(2,1)S(1)}, f32[4,4,...) while((s32[]{:T(128)}, f32[4,4,128]{2,1,0:T(4,128)S(1)}, ...), condition=%wide.region_25.26_spmd, body=%wide.region_24.25_spmd.sunk | while | flops 6295554 | bytes 647461 | solution.py:54
  109.0 3.9 %collective-permute-start.14 = (f32[4,4,128]{2,1,0:T(4,128)S(1)}, f32[4,4,128]{2,1,0:T(4,128)S(1)}, u32[]{:S(2)}, u32[]{:S(2)}) collective-permute-start(f32[4,4,128]{2,1,0:T(4,128)S(1)} %slice_bitcast_fusion.5), channel_id=1, source_target_pairs={{0,8},{8,16},{16,24},{1,9},{9,17},{17,25},{2,10},{10,18},{18,26},{... | collective-permute-start | bytes 24584 | tf_op jit(solution)/shard_map/ppermute | solution.py:28
  114.3 4.7 %while.234 = (s32[]{:T(128)}, f32[4,4,128]{2,1,0:T(4,128)S(1)}, f32[4,4,4,128]{3,2,1,0:T(4,128)S(1)}, bf16[4,4,4,128,128]{4,3,2,1,0:T(8,128)(2,1)S(1)}, f32[4,4,...) while((s32[]{:T(128)}, f32[4,4,128]{2,1,0:T(4,128)S(1)}, ...), condition=%wide.region_27.28_spmd, body=%wide.region_26.27_spmd.sunk | while | flops 6295554 | bytes 647461 | solution.py:54
  119.0 4.2 %collective-permute-start.15 = (f32[4,4,128]{2,1,0:T(4,128)S(1)}, f32[4,4,128]{2,1,0:T(4,128)S(1)}, u32[]{:S(2)}, u32[]{:S(2)}) collective-permute-start(f32[4,4,128]{2,1,0:T(4,128)S(1)} %slice_bitcast_fusion.4), channel_id=1, source_target_pairs={{0,8},{8,16},{16,24},{1,9},{9,17},{17,25},{2,10},{10,18},{18,26},{... | collective-permute-start | bytes 24584 | tf_op jit(solution)/shard_map/ppermute | solution.py:28
  124.6 4.7 %while.235 = (s32[]{:T(128)}, f32[4,4,128]{2,1,0:T(4,128)S(1)}, f32[4,4,4,128]{3,2,1,0:T(4,128)S(1)}, bf16[4,4,4,128,128]{4,3,2,1,0:T(8,128)(2,1)S(1)}, f32[4,4,...) while((s32[]{:T(128)}, f32[4,4,128]{2,1,0:T(4,128)S(1)}, ...), condition=%wide.region_29.30_spmd, body=%wide.region_28.29_spmd.sunk | while | flops 6295554 | bytes 647461 | solution.py:54
  129.3 4.2 %collective-permute-start.16 = (f32[4,4,128]{2,1,0:T(4,128)S(1)}, f32[4,4,128]{2,1,0:T(4,128)S(1)}, u32[]{:S(2)}, u32[]{:S(2)}) collective-permute-start(f32[4,4,128]{2,1,0:T(4,128)S(1)} %slice_bitcast_fusion.3), channel_id=1, source_target_pairs={{0,8},{8,16},{16,24},{1,9},{9,17},{17,25},{2,10},{10,18},{18,26},{... | collective-permute-start | bytes 24584 | tf_op jit(solution)/shard_map/ppermute | solution.py:28
  134.8 4.7 %while.236 = (s32[]{:T(128)}, f32[4,4,128]{2,1,0:T(4,128)S(1)}, f32[4,4,4,128]{3,2,1,0:T(4,128)S(1)}, bf16[4,4,4,128,128]{4,3,2,1,0:T(8,128)(2,1)S(1)}, f32[4,4,...) while((s32[]{:T(128)}, f32[4,4,128]{2,1,0:T(4,128)S(1)}, ...), condition=%wide.region_31.32_spmd, body=%wide.region_30.31_spmd.sunk | while | flops 6295554 | bytes 647461 | solution.py:54
  139.6 4.9 %while.241 = (s32[]{:T(128)}, f32[4,4,128]{2,1,0:T(4,128)S(1)}, f32[4,4,4,128]{3,2,1,0:T(4,128)S(1)}, f32[4,4,4,128]{3,2,1,0:T(4,128)S(1)}, bf16[4,4,4,128,128]{...) while((s32[]{:T(128)}, f32[4,4,128]{2,1,0:T(4,128)S(1)}, ...), condition=%wide.region_33.34_spmd.clone, body=%wide.region_32.33_spmd.clone.sunk | while | flops 6297604 | bytes 655687 | solution.py:68
  145.9 4.3 %collective-permute-done.17 = f32[4,4,128]{2,1,0:T(4,128)S(1)} collective-permute-done((f32[4,4,128]{2,1,0:T(4,128)S(1)}, f32[4,4,128]{2,1,0:T(4,128)S(1)}, u32[]{:S(2)}, u32[]{:S(2)}) %collective-permute-start.17) | collective-permute-done | bytes 8224 | tf_op jit(solution)/shard_map/ppermute | solution.py:28
  150.3 4.8 %while.237 = (s32[]{:T(128)}, f32[4,4,128]{2,1,0:T(4,128)S(1)}, f32[4,4,4,128]{3,2,1,0:T(4,128)S(1)}, f32[4,4,4,128]{3,2,1,0:T(4,128)S(1)}, bf16[4,4,4,128,128]{...) while((s32[]{:T(128)}, f32[4,4,128]{2,1,0:T(4,128)S(1)}, ...), condition=%wide.region_35.36_spmd, body=%wide.region_34.35_spmd.sunk | while | flops 6295555 | bytes 655669 | solution.py:68
  156.4 4.2 %collective-permute-done.18 = f32[4,4,128]{2,1,0:T(4,128)S(1)} collective-permute-done((f32[4,4,128]{2,1,0:T(4,128)S(1)}, f32[4,4,128]{2,1,0:T(4,128)S(1)}, u32[]{:S(2)}, u32[]{:S(2)}) %collective-permute-start.18) | collective-permute-done | bytes 8224 | tf_op jit(solution)/shard_map/ppermute | solution.py:28
  160.7 4.8 %while.238 = (s32[]{:T(128)}, f32[4,4,128]{2,1,0:T(4,128)S(1)}, f32[4,4,4,128]{3,2,1,0:T(4,128)S(1)}, f32[4,4,4,128]{3,2,1,0:T(4,128)S(1)}, bf16[4,4,4,128,128]{...) while((s32[]{:T(128)}, f32[4,4,128]{2,1,0:T(4,128)S(1)}, ...), condition=%wide.region_37.38_spmd, body=%wide.region_36.37_spmd.sunk | while | flops 6295555 | bytes 655669 | solution.py:68
  166.8 4.2 %collective-permute-done.19 = f32[4,4,128]{2,1,0:T(4,128)S(1)} collective-permute-done((f32[4,4,128]{2,1,0:T(4,128)S(1)}, f32[4,4,128]{2,1,0:T(4,128)S(1)}, u32[]{:S(2)}, u32[]{:S(2)}) %collective-permute-start.19) | collective-permute-done | bytes 8224 | tf_op jit(solution)/shard_map/ppermute | solution.py:28
  171.1 4.8 %while.239 = (s32[]{:T(128)}, f32[4,4,128]{2,1,0:T(4,128)S(1)}, f32[4,4,4,128]{3,2,1,0:T(4,128)S(1)}, f32[4,4,4,128]{3,2,1,0:T(4,128)S(1)}, bf16[4,4,4,128,128]{...) while((s32[]{:T(128)}, f32[4,4,128]{2,1,0:T(4,128)S(1)}, ...), condition=%wide.region_39.40_spmd, body=%wide.region_38.39_spmd.sunk | while | flops 6295555 | bytes 655669 | solution.py:68
  180.3 4.2 %collective-permute-start.22 = (f32[4,6,1,128]{3,2,1,0:T(1,128)S(1)}, f32[4,6,1,128]{3,2,1,0:T(1,128)S(1)}, u32[]{:S(2)}, u32[]{:S(2)}) collective-permute-start(f32[4,6,1,128]{3,2,1,0:T(1,128)S(1)} %get-tuple-element.1730), channel_id=1, source_target_pairs={{0,1},{1,2},{2,3},{4,5},{5,6},{6,7},{8,9},{9,10},{10,11},{12,13},{... | collective-permute-start | bytes 36872 | tf_op jit(solution)/shard_map/ppermute | solution.py:19
  192.0 14.8 %all-reduce = f32[64,32]{1,0:T(8,128)S(1)} all-reduce(f32[64,32]{1,0:T(8,128)S(1)} %fusion.179), channel_id=2, replica_groups=mesh['line'=4,'tx'=2,'ty'=4] {'ty'}, use_global_device_ids=true, to_apply=%region_44.45.clone | all-reduce | flops 2048 | bytes 16384
  207.3 8.1 %all_gather.3 = f32[64,32]{1,0:T(8,128)S(1)} all-gather(f32[16,32]{1,0:T(8,128)S(1)} %bitcast.830), channel_id=1, replica_groups=mesh['line'=4,'tx'=2,'ty'=4] {'ty'}, dimensions={0}, use_global_device_ids=true | all-gather | bytes 10240 | tf_op jit(solution)/shard_map/all_gather | solution.py:117
  (389 shorter events, 130.6 us)
Async XLA Ops:
  0.6 12.4 %copy-start = (f32[4,128,128]{2,1,0:T(8,128)S(1)}, f32[4,128,128]{2,1,0:T(8,128)}, u32[]{:S(2)}) copy-start(f32[4,128,128]{2,1,0:T(8,128)} %param.52) | copy-start | bytes 786436
  1.4 5.3 %collective-permute-start = (f32[4,1,4,128]{3,2,1,0:T(4,128)S(1)}, f32[4,1,4,128]{3,2,1,0:T(4,128)S(1)}, u32[]{:S(2)}, u32[]{:S(2)}) collective-permute-start(f32[4,1,4,128]{3,2,1,0:T(4,128)S(1)} %get-tuple-element.1753), channel_id=1, source_target_pairs={{0,4},{1,5},{2,6},{3,7},{8,12},{9,13},{10,14},{11,15},{16,20},{17,... | collective-permute-start | bytes 24584 | tf_op jit(solution)/shard_map/ppermute | solution.py:19
  3.8 3.7 %collective-permute-start.1 = (f32[4,1,4,128]{3,2,1,0:T(4,128)S(1)}, f32[4,1,4,128]{3,2,1,0:T(4,128)S(1)}, u32[]{:S(2)}, u32[]{:S(2)}) collective-permute-start(f32[4,1,4,128]{3,2,1,0:T(4,128)S(1)} %get-tuple-element.1752), channel_id=1, source_target_pairs={{4,0},{5,1},{6,2},{7,3},{12,8},{13,9},{14,10},{15,11},{20,16},{21,... | collective-permute-start | bytes 24584 | tf_op jit(solution)/shard_map/ppermute | solution.py:20
  5.9 11.9 %copy-start.7 = (f32[4,4,4,128]{3,2,1,0:T(4,128)S(1)}, f32[4,4,4,128]{3,2,1,0:T(4,128)}, u32[]{:S(2)}) copy-start(f32[4,4,4,128]{3,2,1,0:T(4,128)} %param.45) | copy-start | bytes 98308
  7.5 8.1 %collective-permute-start.2 = (f32[4,6,1,128]{3,2,1,0:T(1,128)S(1)}, f32[4,6,1,128]{3,2,1,0:T(1,128)S(1)}, u32[]{:S(2)}, u32[]{:S(2)}) collective-permute-start(f32[4,6,1,128]{3,2,1,0:T(1,128)S(1)} %get-tuple-element.1734), channel_id=1, source_target_pairs={{0,1},{1,2},{2,3},{4,5},{5,6},{6,7},{8,9},{9,10},{10,11},{12,13},{... | collective-permute-start | bytes 36872 | tf_op jit(solution)/shard_map/ppermute | solution.py:19
  11.7 5.6 %collective-permute-start.3 = (f32[4,6,1,128]{3,2,1,0:T(1,128)S(1)}, f32[4,6,1,128]{3,2,1,0:T(1,128)S(1)}, u32[]{:S(2)}, u32[]{:S(2)}) collective-permute-start(f32[4,6,1,128]{3,2,1,0:T(1,128)S(1)} %get-tuple-element.1735), channel_id=1, source_target_pairs={{1,0},{2,1},{3,2},{5,4},{6,5},{7,6},{9,8},{10,9},{11,10},{13,12},{... | collective-permute-start | bytes 36872 | tf_op jit(solution)/shard_map/ppermute | solution.py:20
  22.7 4.8 %collective-permute-start.4 = (f32[4,4,128]{2,1,0:T(4,128)S(1)}, f32[4,4,128]{2,1,0:T(4,128)S(1)}, u32[]{:S(2)}, u32[]{:S(2)}) collective-permute-start(f32[4,4,128]{2,1,0:T(4,128)S(1)} %slice_bitcast_fusion.11), channel_id=1, source_target_pairs={{0,8},{8,16},{16,24},{1,9},{9,17},{17,25},{2,10},{10,18},{18,26},{... | collective-permute-start | bytes 24584 | tf_op jit(solution)/shard_map/ppermute | solution.py:28
  32.3 5.6 %collective-permute-start.5 = (f32[4,4,128]{2,1,0:T(4,128)S(1)}, f32[4,4,128]{2,1,0:T(4,128)S(1)}, u32[]{:S(2)}, u32[]{:S(2)}) collective-permute-start(f32[4,4,128]{2,1,0:T(4,128)S(1)} %slice_bitcast_fusion.10), channel_id=1, source_target_pairs={{0,8},{8,16},{16,24},{1,9},{9,17},{17,25},{2,10},{10,18},{18,26},{... | collective-permute-start | bytes 24584 | tf_op jit(solution)/shard_map/ppermute | solution.py:28
  42.5 10.4 %copy-start.3 = (f32[128,128]{1,0:T(8,128)S(1)}, f32[128,128]{1,0:T(8,128)}, u32[]{:S(2)}) copy-start(f32[128,128]{1,0:T(8,128)} %param.51) | copy-start | bytes 196612
  42.5 10.5 %copy-start.5 = (f32[4,4,4]{2,1,0:T(4,128)S(1)}, f32[4,4,4]{2,1,0:T(4,128)}, u32[]{:S(2)}) copy-start(f32[4,4,4]{2,1,0:T(4,128)} %param.49) | copy-start | bytes 772
  42.6 5.7 %collective-permute-start.6 = (f32[4,4,128]{2,1,0:T(4,128)S(1)}, f32[4,4,128]{2,1,0:T(4,128)S(1)}, u32[]{:S(2)}, u32[]{:S(2)}) collective-permute-start(f32[4,4,128]{2,1,0:T(4,128)S(1)} %slice_bitcast_fusion.9), channel_id=1, source_target_pairs={{0,8},{8,16},{16,24},{1,9},{9,17},{17,25},{2,10},{10,18},{18,26},{... | collective-permute-start | bytes 24584 | tf_op jit(solution)/shard_map/ppermute | solution.py:28
  57.9 5.8 %collective-permute-start.7 = (f32[4,4,128]{2,1,0:T(4,128)S(1)}, f32[4,4,128]{2,1,0:T(4,128)S(1)}, u32[]{:S(2)}, u32[]{:S(2)}) collective-permute-start(f32[4,4,128]{2,1,0:T(4,128)S(1)} %slice_bitcast_fusion.8), channel_id=1, source_target_pairs={{8,0},{16,8},{24,16},{9,1},{17,9},{25,17},{10,2},{18,10},{26,18},{... | collective-permute-start | bytes 24584 | tf_op jit(solution)/shard_map/ppermute | solution.py:28
  68.6 5.5 %collective-permute-start.8 = (f32[4,4,128]{2,1,0:T(4,128)S(1)}, f32[4,4,128]{2,1,0:T(4,128)S(1)}, u32[]{:S(2)}, u32[]{:S(2)}) collective-permute-start(f32[4,4,128]{2,1,0:T(4,128)S(1)} %slice_bitcast_fusion.7), channel_id=1, source_target_pairs={{8,0},{16,8},{24,16},{9,1},{17,9},{25,17},{10,2},{18,10},{26,18},{... | collective-permute-start | bytes 24584 | tf_op jit(solution)/shard_map/ppermute | solution.py:28
  78.9 5.5 %collective-permute-start.9 = (f32[4,4,128]{2,1,0:T(4,128)S(1)}, f32[4,4,128]{2,1,0:T(4,128)S(1)}, u32[]{:S(2)}, u32[]{:S(2)}) collective-permute-start(f32[4,4,128]{2,1,0:T(4,128)S(1)} %slice_bitcast_fusion.6), channel_id=1, source_target_pairs={{8,0},{16,8},{24,16},{9,1},{17,9},{25,17},{10,2},{18,10},{26,18},{... | collective-permute-start | bytes 24584 | tf_op jit(solution)/shard_map/ppermute | solution.py:28
  89.3 2.6 %collective-permute-start.10 = (f32[4,1,4,128]{3,2,1,0:T(4,128)S(1)}, f32[4,1,4,128]{3,2,1,0:T(4,128)S(1)}, u32[]{:S(2)}, u32[]{:S(2)}) collective-permute-start(f32[4,1,4,128]{3,2,1,0:T(4,128)S(1)} %get-tuple-element.1747), channel_id=1, source_target_pairs={{0,4},{1,5},{2,6},{3,7},{8,12},{9,13},{10,14},{11,15},{16,20},{17,... | collective-permute-start | bytes 24584 | tf_op jit(solution)/shard_map/ppermute | solution.py:19
  90.6 3.1 %collective-permute-start.11 = (f32[4,1,4,128]{3,2,1,0:T(4,128)S(1)}, f32[4,1,4,128]{3,2,1,0:T(4,128)S(1)}, u32[]{:S(2)}, u32[]{:S(2)}) collective-permute-start(f32[4,1,4,128]{3,2,1,0:T(4,128)S(1)} %get-tuple-element.1746), channel_id=1, source_target_pairs={{4,0},{5,1},{6,2},{7,3},{12,8},{13,9},{14,10},{15,11},{20,16},{21,... | collective-permute-start | bytes 24584 | tf_op jit(solution)/shard_map/ppermute | solution.py:20
  93.7 6.5 %collective-permute-start.12 = (f32[4,6,1,128]{3,2,1,0:T(1,128)S(1)}, f32[4,6,1,128]{3,2,1,0:T(1,128)S(1)}, u32[]{:S(2)}, u32[]{:S(2)}) collective-permute-start(f32[4,6,1,128]{3,2,1,0:T(1,128)S(1)} %get-tuple-element.1732), channel_id=1, source_target_pairs={{0,1},{1,2},{2,3},{4,5},{5,6},{6,7},{8,9},{9,10},{10,11},{12,13},{... | collective-permute-start | bytes 36872 | tf_op jit(solution)/shard_map/ppermute | solution.py:19
  98.0 5.6 %collective-permute-start.13 = (f32[4,6,1,128]{3,2,1,0:T(1,128)S(1)}, f32[4,6,1,128]{3,2,1,0:T(1,128)S(1)}, u32[]{:S(2)}, u32[]{:S(2)}) collective-permute-start(f32[4,6,1,128]{3,2,1,0:T(1,128)S(1)} %get-tuple-element.1733), channel_id=1, source_target_pairs={{1,0},{2,1},{3,2},{5,4},{6,5},{7,6},{9,8},{10,9},{11,10},{13,12},{... | collective-permute-start | bytes 36872 | tf_op jit(solution)/shard_map/ppermute | solution.py:20
  109.0 5.3 %collective-permute-start.14 = (f32[4,4,128]{2,1,0:T(4,128)S(1)}, f32[4,4,128]{2,1,0:T(4,128)S(1)}, u32[]{:S(2)}, u32[]{:S(2)}) collective-permute-start(f32[4,4,128]{2,1,0:T(4,128)S(1)} %slice_bitcast_fusion.5), channel_id=1, source_target_pairs={{0,8},{8,16},{16,24},{1,9},{9,17},{17,25},{2,10},{10,18},{18,26},{... | collective-permute-start | bytes 24584 | tf_op jit(solution)/shard_map/ppermute | solution.py:28
  119.0 5.6 %collective-permute-start.15 = (f32[4,4,128]{2,1,0:T(4,128)S(1)}, f32[4,4,128]{2,1,0:T(4,128)S(1)}, u32[]{:S(2)}, u32[]{:S(2)}) collective-permute-start(f32[4,4,128]{2,1,0:T(4,128)S(1)} %slice_bitcast_fusion.4), channel_id=1, source_target_pairs={{0,8},{8,16},{16,24},{1,9},{9,17},{17,25},{2,10},{10,18},{18,26},{... | collective-permute-start | bytes 24584 | tf_op jit(solution)/shard_map/ppermute | solution.py:28
  129.3 5.6 %collective-permute-start.16 = (f32[4,4,128]{2,1,0:T(4,128)S(1)}, f32[4,4,128]{2,1,0:T(4,128)S(1)}, u32[]{:S(2)}, u32[]{:S(2)}) collective-permute-start(f32[4,4,128]{2,1,0:T(4,128)S(1)} %slice_bitcast_fusion.3), channel_id=1, source_target_pairs={{0,8},{8,16},{16,24},{1,9},{9,17},{17,25},{2,10},{10,18},{18,26},{... | collective-permute-start | bytes 24584 | tf_op jit(solution)/shard_map/ppermute | solution.py:28
  144.4 5.8 %collective-permute-start.17 = (f32[4,4,128]{2,1,0:T(4,128)S(1)}, f32[4,4,128]{2,1,0:T(4,128)S(1)}, u32[]{:S(2)}, u32[]{:S(2)}) collective-permute-start(f32[4,4,128]{2,1,0:T(4,128)S(1)} %slice_bitcast_fusion.2), channel_id=1, source_target_pairs={{8,0},{16,8},{24,16},{9,1},{17,9},{25,17},{10,2},{18,10},{26,18},{... | collective-permute-start | bytes 24584 | tf_op jit(solution)/shard_map/ppermute | solution.py:28
  155.1 5.5 %collective-permute-start.18 = (f32[4,4,128]{2,1,0:T(4,128)S(1)}, f32[4,4,128]{2,1,0:T(4,128)S(1)}, u32[]{:S(2)}, u32[]{:S(2)}) collective-permute-start(f32[4,4,128]{2,1,0:T(4,128)S(1)} %slice_bitcast_fusion.1), channel_id=1, source_target_pairs={{8,0},{16,8},{24,16},{9,1},{17,9},{25,17},{10,2},{18,10},{26,18},{... | collective-permute-start | bytes 24584 | tf_op jit(solution)/shard_map/ppermute | solution.py:28
  165.5 13.4 %copy-start.9 = (s32[4,4,4]{2,1,0:T(4,128)S(1)}, s32[4,4,4]{2,1,0:T(4,128)}, u32[]{:S(2)}) copy-start(s32[4,4,4]{2,1,0:T(4,128)} %param.55) | copy-start | bytes 772
  165.5 13.5 %copy-start.10 = (u32[32]{0:T(128)S(1)}, u32[32]{0:T(128)}, u32[]{:S(2)}) copy-start(u32[32]{0:T(128)} %constant.381) | copy-start | bytes 388
  165.5 5.5 %collective-permute-start.19 = (f32[4,4,128]{2,1,0:T(4,128)S(1)}, f32[4,4,128]{2,1,0:T(4,128)S(1)}, u32[]{:S(2)}, u32[]{:S(2)}) collective-permute-start(f32[4,4,128]{2,1,0:T(4,128)S(1)} %slice_bitcast_fusion), channel_id=1, source_target_pairs={{8,0},{16,8},{24,16},{9,1},{17,9},{25,17},{10,2},{18,10},{26,18},{... | collective-permute-start | bytes 24584 | tf_op jit(solution)/shard_map/ppermute | solution.py:28
  175.9 4.3 %collective-permute-start.20 = (f32[4,1,4,128]{3,2,1,0:T(4,128)S(1)}, f32[4,1,4,128]{3,2,1,0:T(4,128)S(1)}, u32[]{:S(2)}, u32[]{:S(2)}) collective-permute-start(f32[4,1,4,128]{3,2,1,0:T(4,128)S(1)} %get-tuple-element.1744), channel_id=1, source_target_pairs={{0,4},{1,5},{2,6},{3,7},{8,12},{9,13},{10,14},{11,15},{16,20},{17,... | collective-permute-start | bytes 24584 | tf_op jit(solution)/shard_map/ppermute | solution.py:19
  177.2 3.1 %collective-permute-start.21 = (f32[4,1,4,128]{3,2,1,0:T(4,128)S(1)}, f32[4,1,4,128]{3,2,1,0:T(4,128)S(1)}, u32[]{:S(2)}, u32[]{:S(2)}) collective-permute-start(f32[4,1,4,128]{3,2,1,0:T(4,128)S(1)} %get-tuple-element.1745), channel_id=1, source_target_pairs={{4,0},{5,1},{6,2},{7,3},{12,8},{13,9},{14,10},{15,11},{20,16},{21,... | collective-permute-start | bytes 24584 | tf_op jit(solution)/shard_map/ppermute | solution.py:20
  180.3 11.1 %copy-start.8 = (f32[32,128]{1,0:T(8,128)S(1)}, f32[32,128]{1,0:T(8,128)}, u32[]{:S(2)}) copy-start(f32[32,128]{1,0:T(8,128)} %param.56) | copy-start | bytes 49156
  180.3 6.5 %collective-permute-start.22 = (f32[4,6,1,128]{3,2,1,0:T(1,128)S(1)}, f32[4,6,1,128]{3,2,1,0:T(1,128)S(1)}, u32[]{:S(2)}, u32[]{:S(2)}) collective-permute-start(f32[4,6,1,128]{3,2,1,0:T(1,128)S(1)} %get-tuple-element.1730), channel_id=1, source_target_pairs={{0,1},{1,2},{2,3},{4,5},{5,6},{6,7},{8,9},{9,10},{10,11},{12,13},{... | collective-permute-start | bytes 36872 | tf_op jit(solution)/shard_map/ppermute | solution.py:19
  184.5 22.3 %copy-start.6 = (f32[1,1,16,32,32]{4,3,2,1,0:T(8,128)S(1)}, f32[1,1,16,32,32]{4,3,2,1,0:T(8,128)}, u32[]{:S(2)}) copy-start(f32[1,1,16,32,32]{4,3,2,1,0:T(8,128)} %param.57) | copy-start | bytes 196612
  184.5 5.7 %collective-permute-start.23 = (f32[4,6,1,128]{3,2,1,0:T(1,128)S(1)}, f32[4,6,1,128]{3,2,1,0:T(1,128)S(1)}, u32[]{:S(2)}, u32[]{:S(2)}) collective-permute-start(f32[4,6,1,128]{3,2,1,0:T(1,128)S(1)} %get-tuple-element.1731), channel_id=1, source_target_pairs={{1,0},{2,1},{3,2},{5,4},{6,5},{7,6},{9,8},{10,9},{11,10},{13,12},{... | collective-permute-start | bytes 36872 | tf_op jit(solution)/shard_map/ppermute | solution.py:20
  (3 other events, 14.7 us)
where the time goes:
time: 218 us; the launch traced here: 216 us
  matrix products  81.9 us (38%)
  starting transfers between devices  57.8 us (27%)
  waiting for transfers between devices  42.9 us (20%)
  blocking collectives  22.9 us (11%)
  local copies, waits for them, and re-layouts  5.01 us (2%)
  other arithmetic  2.39 us (1%)
    ppermute x12, waiting for transfers between devices, from_behind(): lax.ppermute(value, axis, [(source, source + steps) for source in range(l...  33.9 us
    ppermute x12, starting transfers between devices, from_behind(): lax.ppermute(value, axis, [(source, source + steps) for source in range(l...  32.3 us
    dot_general x32, matrix products, backward_step(): jnp.einsum('xycb,xyb->xyc', inverse.astype(jnp.float32), inner, precision...  29.3 us
    dot_general x32, matrix products, forward_step(): jnp.einsum('xycb,xyb->xyc', inverse.astype(jnp.float32), inner, precision...  29.3 us
    ppermute x6, starting transfers between devices, padded_2(): before = lax.ppermute(last, axis, up)  17.7 us
    unnamed x1, blocking collectives  14.8 us
    ppermute x6, waiting for transfers between devices, padded_2(): after = lax.ppermute(leading, axis, down)  8.93 us
    all_gather x1, blocking collectives, body(): lax.all_gather(update, 'ty', axis=0, tiled=True)  8.12 us
  transfers between devices with their start and end apart: 24, of which 16 were waited for; matrix products, arithmetic and copies ran while one was open for 4% of the time, Pallas kernels for 0%

commit v1 on v0

v1 whole, which is shorter than its diff:
```python
import functools

import jax
import jax.numpy as jnp
from jax import lax
from jax.experimental import pallas as pl
from jax.experimental.pallas import tpu as pltpu
from jax.sharding import PartitionSpec as P

SWEEPS = 2
MESH = pl.DeviceIdType.MESH
F32 = jnp.float32
BF16 = jnp.bfloat16


def split(x):
    hi = x.astype(BF16)
    lo = (x - hi.astype(F32)).astype(BF16)
    return hi, lo


def wide(x):
    return jnp.concatenate(split(x), axis=1)


def tall(x):
    return jnp.concatenate(split(x), axis=0)


def dot(a, b):
    return jnp.dot(a, b, preferred_element_type=F32)


def quadrants(r):
    m, n = r.shape[0] // 2, r.shape[1] // 2
    return (r[:m, :n] + r[m:, :n]) + (r[:m, n:] + r[m:, n:])


def kernel(
    seg, lx, ly, width, owned, cb, n_line, n_tx, n_ty,
    rhs_ref, start_ref, inv_hbm, ls_ref, us_ref, low_ref, upp_ref, fb_ref, kind_ref, scale_ref, agg_ref,
    rm_ref, ci_ref,
    corr_ref, res_ref,
    inv_ref, invt_ref, q_ref, p_ref, ff_ref, f_ref, g_ref, h_ref,
    mask_ref, lu_ref, wf_ref, rmt_ref, rm4_ref, coef_ref, nb0_ref, nb1_ref, nb2_ref, nb3_ref,
    field_ref, diff_ref, base_ref,
    sx_ref, sy_ref, hx_ref, hy_ref, us_buf, ur_buf, ds_buf, dr_buf,
    abuf, cbuf, pbuf, oht_ref, ct_ref,
    inv_sem, hs_sem, hr_sem, uss_sem, usr_sem, dss_sem, dsr_sem, as_sem, ar_sem, cs_sem, cr_sem, ps_sem, pr_sem,
):
    lines = lx * ly
    rows = seg * lines
    line, tx, ty = lax.axis_index("line"), lax.axis_index("tx"), lax.axis_index("ty")
    has = (tx > 0, tx < n_tx - 1, ty > 0, ty < n_ty - 1)

    inv_copy = pltpu.make_async_copy(inv_hbm, inv_ref, inv_sem)
    inv_copy.start()

    def to_peer(o):
        return {"ty": lax.rem(ty + o, n_ty)}

    barrier = pltpu.get_barrier_semaphore()
    near = (
        (has[0], {"tx": tx - 1}), (has[1], {"tx": tx + 1}),
        (line > 0, {"line": line - 1}), (line < n_line - 1, {"line": line + 1}),
    )
    for there, device in near:
        @pl.when(there)
        def _(device=device):
            pl.semaphore_signal(barrier, inc=1, device_id=device, device_id_type=MESH)
    for o in range(1, n_ty):
        pl.semaphore_signal(barrier, inc=1, device_id=to_peer(o), device_id_type=MESH)

    def pack(source, turn):
        for i in range(seg):
            sx_ref[turn, 0, i * ly:(i + 1) * ly] = source[i * lines:i * lines + ly]
            sx_ref[turn, 1, i * ly:(i + 1) * ly] = source[(i + 1) * lines - ly:(i + 1) * lines]
        sy_ref[turn, 0] = source[pl.ds(0, seg * lx, stride=ly), :]
        sy_ref[turn, 1] = source[pl.ds(ly - 1, seg * lx, stride=ly), :]

    def remote(src, dst, ssem, rsem, device):
        return pltpu.make_async_remote_copy(
            src_ref=src, dst_ref=dst, send_sem=ssem, recv_sem=rsem, device_id=device, device_id_type=MESH
        )

    def halo(turn, side):
        send, land = (sx_ref, hx_ref) if side < 2 else (sy_ref, hy_ref)
        step = 1 if side % 2 else -1
        device = {"tx": tx + step} if side < 2 else {"ty": ty + step}
        other = side + 1 - 2 * (side % 2)
        return remote(
            send.at[turn, side % 2], land.at[turn, other % 2], hs_sem.at[turn, side], hr_sem.at[turn, other], device
        )

    def arriving(turn, side):
        send, land = (sx_ref, hx_ref) if side < 2 else (sy_ref, hy_ref)
        device = {"tx": tx} if side < 2 else {"ty": ty}
        return remote(
            send.at[turn, side % 2], land.at[turn, side % 2], hs_sem.at[turn, side], hr_sem.at[turn, side], device
        )

    def send_halos(turn):
        for side in (2, 3, 0, 1):
            @pl.when(has[side])
            def _(side=side):
                halo(turn, side).start()

    def wait_halos(turn):
        for side in (0, 1, 2, 3):
            @pl.when(has[side])
            def _(side=side):
                arriving(turn, side).wait_recv()

    field_ref[...] = start_ref[...]
    pack(field_ref, 0)
    peers = n_ty - 1
    for there, _device in near:
        peers = peers + jnp.where(there, 1, 0)
    pl.semaphore_wait(barrier, peers)
    send_halos(0)

    for side in range(4):
        @pl.when(jnp.logical_not(has[side]))
        def _(side=side):
            land = hx_ref if side < 2 else hy_ref
            for turn in range(SWEEPS + 1):
                land[turn, side % 2] = jnp.zeros(land.shape[2:], F32)

    @pl.loop(0, rows)
    def _(e):
        i = lax.div(e, lines)
        l = lax.rem(e, lines)
        j = lax.div(l, ly)
        k = lax.rem(l, ly)
        for side in range(4):
            value = scale_ref[side, i, j, k]
            kind = kind_ref[side, i, j, k]
            for w in range(4):
                coef_ref[side * 4 + w, pl.ds(e, 1), :] = jnp.full(
                    (1, width), jnp.where(kind == w, value, 0.0), F32
                )
        abuf[0, pl.ds(e, 1), :] = jnp.full((1, width), agg_ref[i, j, k].astype(F32), F32)

    cbuf[0] = ci_ref[...]

    def agg_copy(o):
        return remote(abuf.at[0], abuf.at[o], as_sem.at[o], ar_sem.at[o], to_peer(o))

    def ci_copy(o):
        return remote(cbuf.at[0], cbuf.at[o], cs_sem.at[o], cr_sem.at[o], to_peer(o))

    def proj_copy(o):
        return remote(pbuf.at[0], pbuf.at[o], ps_sem.at[o], pr_sem.at[o], to_peer(o))

    for o in range(1, n_ty):
        agg_copy(o).start()
        ci_copy(o).start()

    row = lax.broadcasted_iota(jnp.int32, (2 * lines, width), 0)
    for l in range(lines):
        chosen = jnp.logical_or(row == l, row == l + lines)
        mask_ref[:, l * width:(l + 1) * width] = jnp.where(chosen, 1.0, 0.0).astype(BF16)
    eye = (
        lax.broadcasted_iota(jnp.int32, (width, width), 0) == lax.broadcasted_iota(jnp.int32, (width, width), 1)
    )
    lu_ref[0:2 * width] = tall(low_ref[...].T)
    lu_ref[2 * width:4 * width] = tall(upp_ref[...].T)
    lu_ref[4 * width:5 * width] = jnp.where(eye, 1.0, 0.0).astype(BF16)
    for w in range(4):
        wf_ref[w * width:(w + 1) * width] = wide(fb_ref[w].T)
    rep = width // cb
    rm4 = jnp.concatenate([rm_ref[...]] * rep, axis=0)
    rm4_ref[...] = wide(rm4)
    rmt_ref[...] = wide(rm4.T)

    inv_copy.wait()

    for i in range(seg):
        @pl.loop(0, lines, unroll=2)
        def _(l, i=i):
            j = lax.div(l, ly)
            k = lax.rem(l, ly)
            r = lax.dot_general(
                lu_ref[...], inv_ref[i, l], (((1,), (1,)), ((), ())), preferred_element_type=F32
            )
            at = pl.ds(pl.multiple_of(l * width, width), width)
            q_ref[i, at, :] = wide(ls_ref[i, j, k] * (r[0:width] + r[width:2 * width]))
            p_ref[i, at, :] = wide(us_ref[i, j, k] * (r[2 * width:3 * width] + r[3 * width:4 * width]))
            if i == 0:
                ff_ref[0, at, :] = -ls_ref[i, j, k] * (r[0:width] + r[width:2 * width])
            if i == seg - 1:
                h = -us_ref[i, j, k] * (r[2 * width:3 * width] + r[3 * width:4 * width])
                h_ref[i, at, :] = wide(h)
            invt_ref[i, at, :] = r[4 * width:5 * width].astype(BF16)

    def forward_maps():
        for i in range(1, seg):
            @pl.loop(0, lines, unroll=4)
            def _(l, i=i):
                at = pl.ds(pl.multiple_of(l * width, width), width)
                ff_ref[i, at, :] = -quadrants(dot(tall(ff_ref[i - 1, at, :]), q_ref[i, at, :]))

        @pl.loop(0, lines, unroll=2)
        def _(l):
            at = pl.ds(pl.multiple_of(l * width, width), width)
            both = wide(ff_ref[seg - 1, at, :])
            f_ref[at, :] = both
            g_ref[seg - 1, at, :] = both

    def backward_maps():
        for i in range(seg - 2, -1, -1):
            @pl.loop(0, lines, unroll=4)
            def _(l, i=i):
                at = pl.ds(pl.multiple_of(l * width, width), width)
                g = g_ref[i + 1, at, :]
                h = h_ref[i + 1, at, :]
                lhs = jnp.concatenate([g[:, :width], g[:, width:], h[:, :width], h[:, width:]], axis=0)
                r = dot(lhs, p_ref[i, at, :])
                g_ref[i, at, :] = wide(ff_ref[i, at, :] - quadrants(r[:2 * width]))
                h_ref[i, at, :] = wide(-quadrants(r[2 * width:]))

    def spread(x):
        return jnp.concatenate([tall(x)] * lines, axis=1) * mask_ref[...]

    def apply(x, weights):
        return quadrants(dot(spread(x), weights))

    def coupled(v, turn):
        wait_halos(turn)
        nb0_ref[...] = pltpu.roll(v, ly, 0)
        nb1_ref[...] = pltpu.roll(v, rows - ly, 0)
        nb2_ref[...] = pltpu.roll(v, 1, 0)
        nb3_ref[...] = pltpu.roll(v, rows - 1, 0)
        for i in range(seg):
            nb0_ref[i * lines:i * lines + ly] = hx_ref[turn, 0, i * ly:(i + 1) * ly]
            nb1_ref[(i + 1) * lines - ly:(i + 1) * lines] = hx_ref[turn, 1, i * ly:(i + 1) * ly]
        nb2_ref[pl.ds(0, seg * lx, stride=ly), :] = hy_ref[turn, 0]
        nb3_ref[pl.ds(ly - 1, seg * lx, stride=ly), :] = hy_ref[turn, 1]
        beside = (nb0_ref[...], nb1_ref[...], nb2_ref[...], nb3_ref[...])
        left = []
        for w in range(4):
            total = coef_ref[w] * beside[0]
            for side in range(1, 4):
                total = total + coef_ref[side * 4 + w] * beside[side]
            left.append(tall(total))
        return quadrants(dot(jnp.concatenate(left, axis=1), wf_ref[...]))

    def up_copy(sweep):
        return remote(us_buf.at[sweep], ur_buf.at[sweep], uss_sem.at[sweep], usr_sem.at[sweep], {"line": line + 1})

    def down_copy(sweep):
        return remote(ds_buf.at[sweep], dr_buf.at[sweep], dss_sem.at[sweep], dsr_sem.at[sweep], {"line": line - 1})

    first, last = line == 0, line == n_line - 1
    late = line >= n_line // 2
    for sweep in range(SWEEPS):
        v = field_ref[...]
        drive = rhs_ref[...] - coupled(v, sweep)
        z = []
        for i in range(seg):
            r = dot(spread(drive[i * lines:(i + 1) * lines]), invt_ref[i])
            z.append(r[:lines] + r[lines:])
            if i > 0:
                z[i] = z[i] - apply(z[i - 1], q_ref[i])

        @pl.when(first)
        def _(sweep=sweep, z=z):
            us_buf[sweep] = z[seg - 1]
            ur_buf[sweep] = jnp.zeros((lines, width), F32)
            if n_line > 1:
                up_copy(sweep).start()

        if sweep == 0:
            forward_maps()
            pl.when(late)(backward_maps)
        w = [None] * seg
        w[seg - 1] = z[seg - 1]
        for i in range(seg - 2, -1, -1):
            w[i] = z[i] - apply(w[i + 1], p_ref[i])
        for i in range(seg):
            base_ref[i] = w[i]

        @pl.when(jnp.logical_not(first))
        def _(sweep=sweep, z=z):
            up_copy(sweep).wait_recv()

            @pl.when(jnp.logical_not(last))
            def _():
                us_buf[sweep] = z[seg - 1] + apply(ur_buf[sweep], f_ref[...])
                up_copy(sweep).start()

        if sweep == 0:
            pl.when(jnp.logical_not(late))(backward_maps)
        incoming = spread(ur_buf[sweep])
        base = base_ref[0] + quadrants(dot(incoming, g_ref[0]))
        base_ref[0] = base

        @pl.when(last)
        def _(sweep=sweep, base=base):
            ds_buf[sweep] = base
            dr_buf[sweep] = jnp.zeros((lines, width), F32)
            if n_line > 1:
                down_copy(sweep).start()

        for i in range(1, seg):
            base_ref[i] = base_ref[i] + quadrants(dot(incoming, g_ref[i]))

        @pl.when(jnp.logical_not(last))
        def _(sweep=sweep):
            down_copy(sweep).wait_recv()

        behind = spread(dr_buf[sweep])
        x = base_ref[0] + quadrants(dot(behind, h_ref[0]))

        @pl.when(jnp.logical_not(jnp.logical_or(first, last)))
        def _(sweep=sweep, x=x):
            ds_buf[sweep] = x
            down_copy(sweep).start()

        field_ref[0:lines] = x
        for i in range(1, seg):
            field_ref[i * lines:(i + 1) * lines] = base_ref[i] + quadrants(dot(behind, h_ref[i]))
        if sweep < SWEEPS - 1:
            pack(field_ref, sweep + 1)
            send_halos(sweep + 1)
        else:
            diff_ref[...] = v - field_ref[...]
            pack(diff_ref, sweep + 1)
            send_halos(sweep + 1)

    aggs = oht_ref.shape[0]
    for o in range(1, n_ty):
        agg_copy(o).wait_recv()
        ci_copy(o).wait_recv()
    for o in range(n_ty):
        ids = abuf[o].T
        for b in range(aggs // width):
            index = lax.broadcasted_iota(jnp.int32, (width, rows), 0) + b * width
            oht_ref[b * width:(b + 1) * width, o * rows:(o + 1) * rows] = jnp.where(
                ids == index.astype(F32), 1.0, 0.0
            ).astype(BF16)
        ct_ref[:, 2 * o * width:2 * (o + 1) * width] = wide(cbuf[o].T)

    residual = coupled(diff_ref[...], SWEEPS)
    res_ref[...] = residual
    pbuf[0] = quadrants(dot(tall(residual), rmt_ref[...]))
    for o in range(1, n_ty):
        proj_copy(o).start()

    a_row = lax.broadcasted_iota(jnp.int32, (aggs, width), 0)
    group = lax.div(lax.broadcasted_iota(jnp.int32, (aggs, width), 1), cb)
    within = lax.rem(a_row, rep)
    own_ids = abuf[0]
    chosen = []
    for b in range(aggs // width):
        index = lax.broadcasted_iota(jnp.int32, (rows, width), 1) + b * width
        chosen.append(jnp.where(own_ids == index.astype(F32), 1.0, 0.0).astype(BF16))
    for o in range(1, n_ty):
        proj_copy(o).wait_recv()
    gathered = wide(pbuf[...].reshape(n_ty * rows, width))
    sums = dot(oht_ref[...], gathered)
    sums = sums[:, :width] + sums[:, width:]
    sums = jnp.where(group == within, sums, 0.0)
    images = dot(tall(sums), ct_ref[...])
    update = jnp.zeros((aggs, width), F32)
    for o in range(n_ty):
        part = quadrants(images[:, 2 * o * width:2 * (o + 1) * width])
        owner = lax.rem(ty + (n_ty - o), n_ty)
        update = update + jnp.where(owner * owned + group * rep + within == a_row, part, 0.0)
    fine = quadrants(dot(tall(update), rm4_ref[...]))
    r = dot(jnp.concatenate(chosen, axis=1), wide(fine))
    corr_ref[...] = field_ref[...] + (r[:, :width] + r[:, width:])

    for turn in range(SWEEPS + 1):
        for side in range(4):
            @pl.when(has[side])
            def _(turn=turn, side=side):
                halo(turn, side).wait_send()
    for sweep in range(SWEEPS):
        @pl.when(jnp.logical_not(last))
        def _(sweep=sweep):
            up_copy(sweep).wait_send()

        @pl.when(jnp.logical_not(first))
        def _(sweep=sweep):
            down_copy(sweep).wait_send()
    for o in range(1, n_ty):
        agg_copy(o).wait_send()
        ci_copy(o).wait_send()
        proj_copy(o).wait_send()


def body(
    right_side, start_field, line_inverse, lower_scale, upper_scale, lower_block, upper_block, face_blocks,
    face_kind, face_scale, agglomerate, restriction, coarse_inverse,
):
    seg, lx, ly, width = right_side.shape
    owned, cb = coarse_inverse.shape[2:4]
    lines = lx * ly
    rows = seg * lines
    n_line, n_tx, n_ty = (lax.axis_size(axis) for axis in ("line", "tx", "ty"))
    rep = width // cb
    groups = owned // rep
    assert rep * cb == width and groups == rep and groups * rep == owned
    aggs = -(-owned * n_ty // width) * width
    blocks = coarse_inverse.reshape(groups, rep, cb, cb).transpose(0, 2, 1, 3).reshape(width, width)
    tall_k = lines * width
    vmem, smem = pl.BlockSpec(memory_space=pltpu.VMEM), pl.BlockSpec(memory_space=pltpu.SMEM)
    dma = pltpu.SemaphoreType.DMA
    turns = SWEEPS + 1
    scratch = [
        pltpu.VMEM((seg, lines, width, width), BF16),
        pltpu.VMEM((seg, tall_k, width), BF16),
        pltpu.VMEM((seg, tall_k, 2 * width), BF16),
        pltpu.VMEM((seg, tall_k, 2 * width), BF16),
        pltpu.VMEM((seg, tall_k, width), F32),
        pltpu.VMEM((tall_k, 2 * width), BF16),
        pltpu.VMEM((seg, tall_k, 2 * width), BF16),
        pltpu.VMEM((seg, tall_k, 2 * width), BF16),
        pltpu.VMEM((2 * lines, tall_k), BF16),
        pltpu.VMEM((5 * width, width), BF16),
        pltpu.VMEM((4 * width, 2 * width), BF16),
        pltpu.VMEM((width, 2 * width), BF16),
        pltpu.VMEM((width, 2 * width), BF16),
        pltpu.VMEM((16, rows, width), F32),
        pltpu.VMEM((rows, width), F32),
        pltpu.VMEM((rows, width), F32),
        pltpu.VMEM((rows, width), F32),
        pltpu.VMEM((rows, width), F32),
        pltpu.VMEM((rows, width), F32),
        pltpu.VMEM((rows, width), F32),
        pltpu.VMEM((seg, lines, width), F32),
        pltpu.VMEM((turns, 2, seg * ly, width), F32),
        pltpu.VMEM((turns, 2, seg * lx, width), F32),
        pltpu.VMEM((turns, 2, seg * ly, width), F32),
        pltpu.VMEM((turns, 2, seg * lx, width), F32),
        pltpu.VMEM((SWEEPS, lines, width), F32),
        pltpu.VMEM((SWEEPS, lines, width), F32),
        pltpu.VMEM((SWEEPS, lines, width), F32),
        pltpu.VMEM((SWEEPS, lines, width), F32),
        pltpu.VMEM((n_ty, rows, width), F32),
        pltpu.VMEM((n_ty, width, width), F32),
        pltpu.VMEM((n_ty, rows, width), F32),
        pltpu.VMEM((aggs, n_ty * rows), BF16),
        pltpu.VMEM((width, 2 * n_ty * width), BF16),
        dma, dma((turns, 4)), dma((turns, 4)),
        dma((SWEEPS,)), dma((SWEEPS,)), dma((SWEEPS,)), dma((SWEEPS,)),
        dma((n_ty,)), dma((n_ty,)), dma((n_ty,)), dma((n_ty,)), dma((n_ty,)), dma((n_ty,)),
    ]
    flat = jax.ShapeDtypeStruct((rows, width), F32)
    corrected, residual = pl.pallas_call(
        functools.partial(kernel, seg, lx, ly, width, owned, cb, n_line, n_tx, n_ty),
        out_shape=(flat, flat),
        in_specs=[
            vmem, vmem, pl.BlockSpec(memory_space=pl.ANY), smem, smem, vmem, vmem, vmem, smem, smem, smem, vmem, vmem,
        ],
        out_specs=(vmem, vmem),
        scratch_shapes=scratch,
        compiler_params=pltpu.CompilerParams(
            collective_id=0, has_side_effects=True, vmem_limit_bytes=60 * 2**20
        ),
    )(
        right_side.reshape(rows, width), start_field.reshape(rows, width),
        line_inverse.reshape(seg, lines, width, width), lower_scale, upper_scale, lower_block, upper_block,
        face_blocks, face_kind, face_scale, agglomerate, restriction, blocks,
    )
    return corrected.reshape(right_side.shape), residual.reshape(right_side.shape)


def solution(mesh):
    in_specs = (
        P("line", "tx", "ty", None),
        P("line", "tx", "ty", None),
        P("line", "tx", "ty", None, None),
        P("line", "tx", "ty"),
        P("line", "tx", "ty"),
        P(),
        P(),
        P(),
        P(None, "line", "tx", "ty"),
        P(None, "line", "tx", "ty"),
        P("line", "tx", "ty"),
        P(),
        P("line", "tx", "ty", None, None),
    )
    out_specs = (P("line", "tx", "ty", None), P("line", "tx", "ty", None))
    return jax.shard_map(body, mesh=mesh, in_specs=in_specs, out_specs=out_specs, check_vma=False)
```

time: 218 us -> 84.4 us (0.39)
  matrix products: 81.9 us -> 0 us
  Pallas kernels: 0 us -> 78.7 us
  starting transfers between devices: 57.8 us -> 0 us
  waiting for transfers between devices: 42.9 us -> 0 us
  blocking collectives: 22.9 us -> 0 us
  other arithmetic: 2.39 us -> 0 us
    dot_general x145 -> x0, matrix products: 81.9 us -> none  [the longest x32 29.3 us: backward_step(): jnp.einsum('xycb,xyb->xyc', inverse.astype(jnp.float32), inner, precision...]
    pallas_call x0 -> x1, Pallas kernels: none -> 78.7 us  [body(): pl.pallas_call(functools.partial(kernel, seg, lx, ly, width, owned, cb, n...]
    ppermute x24 -> x0, starting transfers between devices: 57.8 us -> none  [the longest x12 32.3 us: from_behind(): lax.ppermute(value, axis, [(source, source + steps) for source in range(l...]
    ppermute x24 -> x0, waiting for transfers between devices: 42.9 us -> none  [the longest x12 33.9 us: from_behind(): lax.ppermute(value, axis, [(source, source + steps) for source in range(l...]
    unnamed x1 -> x0, blocking collectives: 14.8 us -> none
    all_gather x1 -> x0, blocking collectives: 8.12 us -> none  [body(): lax.all_gather(update, 'ty', axis=0, tiled=True)]
  transfers between devices with their start and end apart: 24 -> 0, of which waited for: 16 -> 0; matrix products, arithmetic and copies ran while one was open for 4% -> 0% of each run, Pallas kernels for 0% -> 0%
where the time goes in v1:
time: 84.4 us; the launch traced here: 84 us
  Pallas kernels  78.7 us (93%)
  local copies, waits for them, and re-layouts  4.65 us (6%)
    pallas_call x1, Pallas kernels, body(): pl.pallas_call(functools.partial(kernel, seg, lx, ly, width, owned, cb, n...  78.7 us
    unnamed x2, local copies, waits for them, and re-layouts  2.75 us
    reshape x2, local copies, waits for them, and re-layouts, body(): coarse_inverse.reshape(groups, rep, cb, cb).transpose(0, 2, 1, 3)  1.9 us

profile of v1, /device:TPU:0, one launch (start us, length us, event | category | flops | bytes accessed | tf_op | source)
XLA Modules:
  0.0 84.0 jit_solution(12038895222524333060)
XLA Ops:
  0.6 1.1 %copy.17 = f32[4,4,32,32]{3,1,2,0:T(4,128)S(1)} copy(f32[4,4,32,32]{3,2,1,0:T(8,128)} %bitcast.11) | data formatting | bytes 131072 | tf_op jit(solution)/shard_map/reshape | solution.py:406
  1.8 0.8 reshape.29.ci_ref
  2.5 78.7 %shard_map.140 = (f32[64,128]{1,0:T(8,128)}, f32[64,128]{1,0:T(8,128)}) custom-call(f32[64,128]{1,0:T(8,128)} %bitcast.12, f32[64,128]{1,0:T(8,128)} %bitcast.13, bf16[4,16,128,128]{3,2,1,0:T(8,128)(2,1)} %bitcast.9, f32[4,4,4]{2,1,0:T(4,128)} %ls_ref.1, f32[4,4,4]{2,1,0:T(4,128)} %us_ref.1, f32[128,128]{1,0:T(8,128)} %low_ref.1, f32[128,128]{1,0:T(8,128)} %upp_ref.1, ...), custom_call_target="tpu_custom_call" | custom-call | tf_op jit(solution)/shard_map/pallas_call | solution.py:451
  81.3 1.4 %copy.20 = f32[4,4,4,128]{3,2,1,0:T(4,128)} copy(f32[4,4,4,128]{3,2,1,0:T(4,128)} %bitcast.15) | data formatting | bytes 65536
  82.7 1.4 %copy.21 = f32[4,4,4,128]{3,2,1,0:T(4,128)} copy(f32[4,4,4,128]{3,2,1,0:T(4,128)} %bitcast.14) | data formatting | bytes 65536

commit v2 on v1

--- a/solution.py
+++ b/solution.py
@@ -126,7 +126,7 @@
             for turn in range(SWEEPS + 1):
                 land[turn, side % 2] = jnp.zeros(land.shape[2:], F32)
 
-    @pl.loop(0, rows)
+    @pl.loop(0, rows, unroll=4)
     def _(e):
         i = lax.div(e, lines)
         l = lax.rem(e, lines)
@@ -141,7 +141,16 @@
                 )
         abuf[0, pl.ds(e, 1), :] = jnp.full((1, width), agg_ref[i, j, k].astype(F32), F32)
 
-    cbuf[0] = ci_ref[...]
+    rep = width // cb
+    placed = jnp.zeros((width, width), F32)
+    for a in range(rep):
+        stacked = jnp.concatenate([ci_ref[t * rep + a] for t in range(rep)], axis=0)
+        lane = lax.broadcasted_iota(jnp.int32, (cb, width), 1)
+        place = lane == lax.broadcasted_iota(jnp.int32, (cb, width), 0) + a * cb
+        place = jnp.where(place, 1.0, 0.0).astype(BF16)
+        for half in split(stacked):
+            placed = placed + dot(half, place)
+    cbuf[0] = placed
 
     def agg_copy(o):
         return remote(abuf.at[0], abuf.at[o], as_sem.at[o], ar_sem.at[o], to_peer(o))
@@ -163,61 +172,77 @@
     eye = (
         lax.broadcasted_iota(jnp.int32, (width, width), 0) == lax.broadcasted_iota(jnp.int32, (width, width), 1)
     )
-    lu_ref[0:2 * width] = tall(low_ref[...].T)
-    lu_ref[2 * width:4 * width] = tall(upp_ref[...].T)
-    lu_ref[4 * width:5 * width] = jnp.where(eye, 1.0, 0.0).astype(BF16)
+    lu_ref[0:width] = wide(low_ref[...].T)
+    lu_ref[width:2 * width, :width] = jnp.where(eye, 1.0, 0.0).astype(BF16)
+    lu_ref[width:2 * width, width:] = jnp.zeros((width, width), BF16)
+    lu_ref[2 * width:3 * width] = wide(upp_ref[...].T)
     for w in range(4):
         wf_ref[w * width:(w + 1) * width] = wide(fb_ref[w].T)
-    rep = width // cb
     rm4 = jnp.concatenate([rm_ref[...]] * rep, axis=0)
     rm4_ref[...] = wide(rm4)
     rmt_ref[...] = wide(rm4.T)
 
     inv_copy.wait()
 
+    def at(l):
+        return pl.ds(pl.multiple_of(l * width, width), width)
+
+    def folded(i, l, left):
+        pair = jnp.concatenate([inv_ref[i, l], inv_ref[i, l + 1]], axis=0)
+        pair = jnp.concatenate([pair, pair], axis=1)
+        return lax.dot_general(left, pair, (((1,), (1,)), ((), ())), preferred_element_type=F32)
+
+    def halves(r):
+        return r[:, :width] + r[:, width:]
+
+    def stacked_twice(w):
+        return jnp.concatenate([w, w], axis=0)
+
     for i in range(seg):
-        @pl.loop(0, lines, unroll=2)
-        def _(l, i=i):
-            j = lax.div(l, ly)
-            k = lax.rem(l, ly)
-            r = lax.dot_general(
-                lu_ref[...], inv_ref[i, l], (((1,), (1,)), ((), ())), preferred_element_type=F32
-            )
-            at = pl.ds(pl.multiple_of(l * width, width), width)
-            q_ref[i, at, :] = wide(ls_ref[i, j, k] * (r[0:width] + r[width:2 * width]))
-            p_ref[i, at, :] = wide(us_ref[i, j, k] * (r[2 * width:3 * width] + r[3 * width:4 * width]))
-            if i == 0:
-                ff_ref[0, at, :] = -ls_ref[i, j, k] * (r[0:width] + r[width:2 * width])
-            if i == seg - 1:
-                h = -us_ref[i, j, k] * (r[2 * width:3 * width] + r[3 * width:4 * width])
-                h_ref[i, at, :] = wide(h)
-            invt_ref[i, at, :] = r[4 * width:5 * width].astype(BF16)
+        @pl.loop(0, lines // 2, unroll=2)
+        def _(pair, i=i):
+            r = folded(i, pair * 2, lu_ref[0:2 * width])
+            for m in range(2):
+                l = pair * 2 + m
+                scale = ls_ref[i, lax.div(l, ly), lax.rem(l, ly)]
+                q = scale * r[:width, m * width:(m + 1) * width]
+                q_ref[i, at(l), :] = wide(q)
+                if i == 0:
+                    ff_ref[0, at(l), :] = -q
+                invt_ref[i, at(l), :] = r[width:, m * width:(m + 1) * width].astype(BF16)
+
+    def upper_maps():
+        for i in range(seg):
+            @pl.loop(0, lines // 2, unroll=2)
+            def _(pair, i=i):
+                r = folded(i, pair * 2, lu_ref[2 * width:3 * width])
+                for m in range(2):
+                    l = pair * 2 + m
+                    scale = us_ref[i, lax.div(l, ly), lax.rem(l, ly)]
+                    p = scale * r[:, m * width:(m + 1) * width]
+                    p_ref[i, at(l), :] = wide(p)
+                    if i == seg - 1:
+                        h_ref[i, at(l), :] = wide(-p)
 
     def forward_maps():
         for i in range(1, seg):
             @pl.loop(0, lines, unroll=4)
             def _(l, i=i):
-                at = pl.ds(pl.multiple_of(l * width, width), width)
-                ff_ref[i, at, :] = -quadrants(dot(tall(ff_ref[i - 1, at, :]), q_ref[i, at, :]))
-
-        @pl.loop(0, lines, unroll=2)
-        def _(l):
-            at = pl.ds(pl.multiple_of(l * width, width), width)
-            both = wide(ff_ref[seg - 1, at, :])
-            f_ref[at, :] = both
-            g_ref[seg - 1, at, :] = both
+                f = -halves(dot(wide(ff_ref[i - 1, at(l), :]), stacked_twice(q_ref[i, at(l), :])))
+                ff_ref[i, at(l), :] = f
+                if i == seg - 1:
+                    both = wide(f)
+                    f_ref[at(l), :] = both
+                    g_ref[i, at(l), :] = both
 
     def backward_maps():
         for i in range(seg - 2, -1, -1):
             @pl.loop(0, lines, unroll=4)
             def _(l, i=i):
-                at = pl.ds(pl.multiple_of(l * width, width), width)
-                g = g_ref[i + 1, at, :]
-                h = h_ref[i + 1, at, :]
-                lhs = jnp.concatenate([g[:, :width], g[:, width:], h[:, :width], h[:, width:]], axis=0)
-                r = dot(lhs, p_ref[i, at, :])
-                g_ref[i, at, :] = wide(ff_ref[i, at, :] - quadrants(r[:2 * width]))
-                h_ref[i, at, :] = wide(-quadrants(r[2 * width:]))
+                left = jnp.concatenate([g_ref[i + 1, at(l), :], h_ref[i + 1, at(l), :]], axis=0)
+                r = halves(dot(left, stacked_twice(p_ref[i, at(l), :])))
+                g_ref[i, at(l), :] = wide(ff_ref[i, at(l), :] - r[:width])
+                h_ref[i, at(l), :] = wide(-r[width:])
 
     def spread(x):
         return jnp.concatenate([tall(x)] * lines, axis=1) * mask_ref[...]
@@ -253,9 +278,64 @@
 
     first, last = line == 0, line == n_line - 1
     late = line >= n_line // 2
-    for sweep in range(SWEEPS):
-        v = field_ref[...]
-        drive = rhs_ref[...] - coupled(v, sweep)
+    def early(sweep):
+        drive = rhs_ref[...] - coupled(field_ref[...], sweep)
+        for i in range(seg):
+            r = dot(spread(drive[i * lines:(i + 1) * lines]), invt_ref[i])
+            base_ref[i] = r[:lines] + r[lines:]
+
+        @pl.when(late)
+        def _():
+            upper_maps()
+            forward_maps()
+
+        pl.when(last)(backward_maps)
+
+        @pl.when(first)
+        def _():
+            ur_buf[sweep] = jnp.zeros((lines, width), F32)
+
+        @pl.when(jnp.logical_not(first))
+        def _():
+            up_copy(sweep).wait_recv()
+
+        y = ur_buf[sweep]
+        for i in range(seg):
+            y = base_ref[i] - apply(y, q_ref[i])
+            base_ref[i] = y
+
+        @pl.when(jnp.logical_not(last))
+        def _():
+            us_buf[sweep] = y
+            up_copy(sweep).start()
+
+        @pl.when(jnp.logical_not(late))
+        def _():
+            upper_maps()
+            forward_maps()
+
+        pl.when(jnp.logical_not(last))(backward_maps)
+
+        @pl.when(last)
+        def _():
+            dr_buf[sweep] = jnp.zeros((lines, width), F32)
+
+        @pl.when(jnp.logical_not(last))
+        def _():
+            down_copy(sweep).wait_recv()
+
+        x = dr_buf[sweep]
+        for i in range(seg - 1, -1, -1):
+            x = base_ref[i] - apply(x, p_ref[i])
+            field_ref[i * lines:(i + 1) * lines] = x
+
+        @pl.when(jnp.logical_not(first))
+        def _():
+            ds_buf[sweep] = x
+            down_copy(sweep).start()
+
+    def mapped(sweep):
+        drive = rhs_ref[...] - coupled(field_ref[...], sweep)
         z = []
         for i in range(seg):
             r = dot(spread(drive[i * lines:(i + 1) * lines]), invt_ref[i])
@@ -264,15 +344,12 @@
                 z[i] = z[i] - apply(z[i - 1], q_ref[i])
 
         @pl.when(first)
-        def _(sweep=sweep, z=z):
+        def _():
             us_buf[sweep] = z[seg - 1]
             ur_buf[sweep] = jnp.zeros((lines, width), F32)
             if n_line > 1:
                 up_copy(sweep).start()
 
-        if sweep == 0:
-            forward_maps()
-            pl.when(late)(backward_maps)
         w = [None] * seg
         w[seg - 1] = z[seg - 1]
         for i in range(seg - 2, -1, -1):
@@ -281,7 +358,7 @@
             base_ref[i] = w[i]
 
         @pl.when(jnp.logical_not(first))
-        def _(sweep=sweep, z=z):
+        def _():
             up_copy(sweep).wait_recv()
 
             @pl.when(jnp.logical_not(last))
@@ -289,14 +366,12 @@
                 us_buf[sweep] = z[seg - 1] + apply(ur_buf[sweep], f_ref[...])
                 up_copy(sweep).start()
 
-        if sweep == 0:
-            pl.when(jnp.logical_not(late))(backward_maps)
         incoming = spread(ur_buf[sweep])
         base = base_ref[0] + quadrants(dot(incoming, g_ref[0]))
         base_ref[0] = base
 
         @pl.when(last)
-        def _(sweep=sweep, base=base):
+        def _():
             ds_buf[sweep] = base
             dr_buf[sweep] = jnp.zeros((lines, width), F32)
             if n_line > 1:
@@ -306,20 +381,24 @@
             base_ref[i] = base_ref[i] + quadrants(dot(incoming, g_ref[i]))
 
         @pl.when(jnp.logical_not(last))
-        def _(sweep=sweep):
+        def _():
             down_copy(sweep).wait_recv()
 
         behind = spread(dr_buf[sweep])
         x = base_ref[0] + quadrants(dot(behind, h_ref[0]))
 
         @pl.when(jnp.logical_not(jnp.logical_or(first, last)))
-        def _(sweep=sweep, x=x):
+        def _():
             ds_buf[sweep] = x
             down_copy(sweep).start()
 
         field_ref[0:lines] = x
         for i in range(1, seg):
             field_ref[i * lines:(i + 1) * lines] = base_ref[i] + quadrants(dot(behind, h_ref[i]))
+
+    for sweep in range(SWEEPS):
+        v = field_ref[...]
+        (early if sweep == 0 else mapped)(sweep)
         if sweep < SWEEPS - 1:
             pack(field_ref, sweep + 1)
             send_halos(sweep + 1)
@@ -403,7 +482,6 @@
     groups = owned // rep
     assert rep * cb == width and groups == rep and groups * rep == owned
     aggs = -(-owned * n_ty // width) * width
-    blocks = coarse_inverse.reshape(groups, rep, cb, cb).transpose(0, 2, 1, 3).reshape(width, width)
     tall_k = lines * width
     vmem, smem = pl.BlockSpec(memory_space=pltpu.VMEM), pl.BlockSpec(memory_space=pltpu.SMEM)
     dma = pltpu.SemaphoreType.DMA
@@ -418,7 +496,7 @@
         pltpu.VMEM((seg, tall_k, 2 * width), BF16),
         pltpu.VMEM((seg, tall_k, 2 * width), BF16),
         pltpu.VMEM((2 * lines, tall_k), BF16),
-        pltpu.VMEM((5 * width, width), BF16),
+        pltpu.VMEM((3 * width, 2 * width), BF16),
         pltpu.VMEM((4 * width, 2 * width), BF16),
         pltpu.VMEM((width, 2 * width), BF16),
         pltpu.VMEM((width, 2 * width), BF16),
@@ -462,7 +540,8 @@
     )(
         right_side.reshape(rows, width), start_field.reshape(rows, width),
         line_inverse.reshape(seg, lines, width, width), lower_scale, upper_scale, lower_block, upper_block,
-        face_blocks, face_kind, face_scale, agglomerate, restriction, blocks,
+        face_blocks, face_kind, face_scale, agglomerate, restriction,
+        coarse_inverse.reshape(owned, cb, cb),
     )
     return corrected.reshape(right_side.shape), residual.reshape(right_side.shape)
 

time: 84.4 us -> 81.2 us (0.962)
  local copies, waits for them, and re-layouts: 4.65 us -> 2.75 us
  Pallas kernels: 78.7 us -> 77.4 us
    reshape x2 -> x0, local copies, waits for them, and re-layouts: 1.9 us -> none  [body(): coarse_inverse.reshape(groups, rep, cb, cb).transpose(0, 2, 1, 3)]
    pallas_call x1, Pallas kernels: 78.7 us -> 77.4 us  [body(): pl.pallas_call(functools.partial(kernel, seg, lx, ly, width, owned, cb, n...]
where the time goes in v2:
time: 81.2 us; the launch traced here: 80.8 us
  Pallas kernels  77.4 us (95%)
  local copies, waits for them, and re-layouts  2.75 us (3%)
    pallas_call x1, Pallas kernels, body(): pl.pallas_call(functools.partial(kernel, seg, lx, ly, width, owned, cb, n...  77.4 us
    unnamed x2, local copies, waits for them, and re-layouts  2.75 us

profile of v2, /device:TPU:0, one launch (start us, length us, event | category | flops | bytes accessed | tf_op | source)
XLA Modules:
  0.0 80.8 jit_solution(3209052088266689337)
XLA Ops:
  0.6 77.4 %shard_map.140 = (f32[64,128]{1,0:T(8,128)}, f32[64,128]{1,0:T(8,128)}) custom-call(f32[64,128]{1,0:T(8,128)} %bitcast.8, f32[64,128]{1,0:T(8,128)} %bitcast.9, bf16[4,16,128,128]{3,2,1,0:T(8,128)(2,1)} %bitcast.6, f32[4,4,4]{2,1,0:T(4,128)} %ls_ref.1, f32[4,4,4]{2,1,0:T(4,128)} %us_ref.1, f32[128,128]{1,0:T(8,128)} %low_ref.1, f32[128,128]{1,0:T(8,128)} %upp_ref.1, ...), custom_call_target="tpu_custom_call" | custom-call | tf_op jit(solution)/shard_map/pallas_call | solution.py:529
  78.1 1.4 %copy.17 = f32[4,4,4,128]{3,2,1,0:T(4,128)} copy(f32[4,4,4,128]{3,2,1,0:T(4,128)} %bitcast.11) | data formatting | bytes 65536
  79.5 1.4 %copy.18 = f32[4,4,4,128]{3,2,1,0:T(4,128)} copy(f32[4,4,4,128]{3,2,1,0:T(4,128)} %bitcast.10) | data formatting | bytes 65536

commit v3 on v2

--- a/solution.py
+++ b/solution.py
@@ -113,12 +113,6 @@
 
     field_ref[...] = start_ref[...]
     pack(field_ref, 0)
-    peers = n_ty - 1
-    for there, _device in near:
-        peers = peers + jnp.where(there, 1, 0)
-    pl.semaphore_wait(barrier, peers)
-    send_halos(0)
-
     for side in range(4):
         @pl.when(jnp.logical_not(has[side]))
         def _(side=side):
@@ -140,6 +134,12 @@
                     (1, width), jnp.where(kind == w, value, 0.0), F32
                 )
         abuf[0, pl.ds(e, 1), :] = jnp.full((1, width), agg_ref[i, j, k].astype(F32), F32)
+
+    peers = n_ty - 1
+    for there, _device in near:
+        peers = peers + jnp.where(there, 1, 0)
+    pl.semaphore_wait(barrier, peers)
+    send_halos(0)
 
     rep = width // cb
     placed = jnp.zeros((width, width), F32)
@@ -278,6 +278,23 @@
 
     first, last = line == 0, line == n_line - 1
     late = line >= n_line // 2
+    def from_above(sweep):
+        @pl.when(jnp.logical_not(last))
+        def _():
+            down_copy(sweep).wait_recv()
+
+        behind = spread(dr_buf[sweep])
+        x = base_ref[0] + quadrants(dot(behind, h_ref[0]))
+
+        @pl.when(jnp.logical_not(jnp.logical_or(first, last)))
+        def _():
+            ds_buf[sweep] = x
+            down_copy(sweep).start()
+
+        field_ref[0:lines] = x
+        for i in range(1, seg):
+            field_ref[i * lines:(i + 1) * lines] = base_ref[i] + quadrants(dot(behind, h_ref[i]))
+
     def early(sweep):
         drive = rhs_ref[...] - coupled(field_ref[...], sweep)
         for i in range(seg):
@@ -316,23 +333,19 @@
 
         pl.when(jnp.logical_not(last))(backward_maps)
 
+        b = base_ref[seg - 1]
+        for i in range(seg - 2, -1, -1):
+            b = base_ref[i] - apply(b, p_ref[i])
+            base_ref[i] = b
+
         @pl.when(last)
         def _():
+            ds_buf[sweep] = b
             dr_buf[sweep] = jnp.zeros((lines, width), F32)
-
-        @pl.when(jnp.logical_not(last))
-        def _():
-            down_copy(sweep).wait_recv()
-
-        x = dr_buf[sweep]
-        for i in range(seg - 1, -1, -1):
-            x = base_ref[i] - apply(x, p_ref[i])
-            field_ref[i * lines:(i + 1) * lines] = x
-
-        @pl.when(jnp.logical_not(first))
-        def _():
-            ds_buf[sweep] = x
-            down_copy(sweep).start()
+            if n_line > 1:
+                down_copy(sweep).start()
+
+        from_above(sweep)
 
     def mapped(sweep):
         drive = rhs_ref[...] - coupled(field_ref[...], sweep)
@@ -380,21 +393,7 @@
         for i in range(1, seg):
             base_ref[i] = base_ref[i] + quadrants(dot(incoming, g_ref[i]))
 
-        @pl.when(jnp.logical_not(last))
-        def _():
-            down_copy(sweep).wait_recv()
-
-        behind = spread(dr_buf[sweep])
-        x = base_ref[0] + quadrants(dot(behind, h_ref[0]))
-
-        @pl.when(jnp.logical_not(jnp.logical_or(first, last)))
-        def _():
-            ds_buf[sweep] = x
-            down_copy(sweep).start()
-
-        field_ref[0:lines] = x
-        for i in range(1, seg):
-            field_ref[i * lines:(i + 1) * lines] = base_ref[i] + quadrants(dot(behind, h_ref[i]))
+        from_above(sweep)
 
     for sweep in range(SWEEPS):
         v = field_ref[...]

time: 81.2 us -> 76.8 us (0.946)
  Pallas kernels: 77.4 us -> 73 us
    pallas_call x1, Pallas kernels: 77.4 us -> 73 us  [body(): pl.pallas_call(functools.partial(kernel, seg, lx, ly, width, owned, cb, n...]
where the time goes in v3:
time: 76.8 us; the launch traced here: 76.4 us
  Pallas kernels  73 us (95%)
  local copies, waits for them, and re-layouts  2.75 us (4%)
    pallas_call x1, Pallas kernels, body(): pl.pallas_call(functools.partial(kernel, seg, lx, ly, width, owned, cb, n...  73 us
    unnamed x2, local copies, waits for them, and re-layouts  2.75 us

profile of v3, /device:TPU:0, one launch (start us, length us, event | category | flops | bytes accessed | tf_op | source)
XLA Modules:
  0.0 76.4 jit_solution(14885977644288324205)
XLA Ops:
  0.6 73.0 %shard_map.140 = (f32[64,128]{1,0:T(8,128)}, f32[64,128]{1,0:T(8,128)}) custom-call(f32[64,128]{1,0:T(8,128)} %bitcast.8, f32[64,128]{1,0:T(8,128)} %bitcast.9, bf16[4,16,128,128]{3,2,1,0:T(8,128)(2,1)} %bitcast.6, f32[4,4,4]{2,1,0:T(4,128)} %ls_ref.1, f32[4,4,4]{2,1,0:T(4,128)} %us_ref.1, f32[128,128]{1,0:T(8,128)} %low_ref.1, f32[128,128]{1,0:T(8,128)} %upp_ref.1, ...), custom_call_target="tpu_custom_call" | custom-call | tf_op jit(solution)/shard_map/pallas_call | solution.py:528
  73.7 1.4 %copy.17 = f32[4,4,4,128]{3,2,1,0:T(4,128)} copy(f32[4,4,4,128]{3,2,1,0:T(4,128)} %bitcast.11) | data formatting | bytes 65536
  75.0 1.4 %copy.18 = f32[4,4,4,128]{3,2,1,0:T(4,128)} copy(f32[4,4,4,128]{3,2,1,0:T(4,128)} %bitcast.10) | data formatting | bytes 65536
